TPU v7x, 512 devices: a whole 4x8x8 slice. The times are simulated.
512 devices in a mesh: tm: 64 (over z_hi, x, y), space: 8 (over z_lo, core).
Axes of the slice: x: 4, y: 8, z: 8 (z_hi: 2, z_lo: 4; z = z_hi * 4 + z_lo), core: 2. Of those that a mesh axis runs over, the one named last changes fastest.
Arguments:
- start_states: float32 [64, 128, 16, 128], P('tm', 'space'), may hold values from -6 to 6
- material: int32 [128, 16, 128], P('space'), may hold values from 0 to 15
- source: float32 [128, 16, 128], P('space'), may hold values from -0.6 to 0.6
- conductivity: float32 [16], replicated, may hold values from 0.02 to 0.16
- tide_amp: float32 [12], replicated, may hold values from -1.5 to 1.5
- phase: int32 [64], P('tm'), may hold values from 0 to 11
- coarse_rate: float32 [32, 4, 32], P('space'), may hold values from 0.3 to 40
Outputs:
- final_states: float32 [64, 128, 16, 128], P('tm', 'space')
All inputs are finite; a program needn't handle non-finite values.
Results may differ from a plain program's by a relative error of at most 0.00013.
Values sent between devices are 32-bit elements; how exact they have to be, the bound alone decides.
A program may use at most 64 MiB of HBM per device.

v0:
```python
import jax
import jax.numpy as jnp
from jax import lax
from jax.sharding import PartitionSpec as P

FINE = 10
ITERS = 2


def padded_2(block, sides, width):
    for axis, dim in sides:
        count = lax.axis_size(axis)
        forward = [(i, i + 1) for i in range(count - 1)]
        backward = [(target, source) for source, target in forward]
        low = lax.ppermute(
            lax.slice_in_dim(block, block.shape[dim] - width, None, axis=dim), axis, forward
        )
        high = lax.ppermute(lax.slice_in_dim(block, 0, width, axis=dim), axis, backward)
        block = jnp.concatenate([low, block, high], axis=dim)
    return block


def from_behind(block, axis, distance):
    devices = range(lax.axis_size(axis))
    route = [((i - distance) % len(devices), i) for i in devices]
    return lax.ppermute(block, axis, route)


def lookup_coef(material, conductivity):
    result = jnp.zeros(material.shape, jnp.float32)
    for class_id in range(conductivity.shape[0]):
        result = jnp.where(material == class_id, conductivity[class_id], result)
    return result


def neighbour_total(padded):
    framed = jnp.pad(padded, ((0, 0), (1, 1), (1, 1)))
    total = framed[2:, 1:-1, 1:-1] + framed[:-2, 1:-1, 1:-1]
    total = total + framed[1:-1, 2:, 1:-1] + framed[1:-1, :-2, 1:-1]
    total = total + framed[1:-1, 1:-1, 2:] + framed[1:-1, 1:-1, :-2]
    return total


def slab_update(field_now, cell_coef, forcing):
    padded = padded_2(field_now, (("space", 0),), 1)
    neighbours = neighbour_total(padded)
    return field_now + cell_coef * (neighbours - 6.0 * field_now) + forcing


def restrict(field_now):
    depth, rows, cols = field_now.shape
    blocks = field_now.reshape((depth // 4, 4, rows // 4, 4, cols // 4, 4))
    return blocks.mean(axis=(1, 3, 5))


def prolong(coarse):
    depth, rows, cols = coarse.shape
    wide = jnp.broadcast_to(coarse[:, None, :, None, :, None], (depth, 4, rows, 4, cols, 4))
    return wide.reshape((depth * 4, rows * 4, cols * 4))


def body(start_states, material, source, conductivity, tide_amp, phase, coarse_rate):
    windows = lax.axis_size("tm")
    device_index = lax.axis_index("tm")
    cell_coef = lookup_coef(material, conductivity)
    phase_ids = jnp.arange(tide_amp.shape[0], dtype=jnp.int32)
    decay = jnp.exp(-coarse_rate / windows)
    closure = 1.0 - jnp.exp(-coarse_rate)
    field_now = start_states[0]
    for outer in range(ITERS):
        tide_level = jnp.sum(jnp.where(phase_ids == phase[0], tide_amp, 0.0))
        forcing = tide_level * source
        finish = field_now
        for substep in range(FINE):
            finish = slab_update(finish, cell_coef, forcing)
        coarse_start = restrict(field_now)
        jump_now = restrict(finish) - decay * coarse_start
        pieces = lax.all_gather(jump_now[None], "tm", axis=0, tiled=True)
        count = pieces.shape[0]
        seen = jnp.arange(count, dtype=jnp.int32)
        lagged = (device_index - 1 - seen) % windows
        weights = jnp.exp(
            -coarse_rate[None] * lagged.astype(jnp.float32)[:, None, None, None] / windows
        )
        gathered_sum = jnp.sum(weights * pieces, axis=0)
        coarse = gathered_sum / closure
        corrected = finish + prolong(decay * (coarse - coarse_start))
        field_now = from_behind(corrected, "tm", 1)
    return field_now[None]


def solution(mesh):
    placed = (
        P("tm", "space", None, None),
        P("space", None, None),
        P("space", None, None),
        P(),
        P(),
        P("tm"),
        P("space", None, None),
    )
    return jax.shard_map(
        body, mesh=mesh, in_specs=placed, out_specs=P("tm", "space", None, None), check_vma=False
    )
```

profile of v0, /device:TPU:64, one launch (start us, length us, event | category | flops | bytes accessed | tf_op | source)
XLA Modules:
  0.0 887.4 jit_solution(9521776563705246436)
XLA Ops:
  2.7 3.6 collective-permute-start
  11.3 11.9 %fusion.101 = f32[16,16,128]{2,1,0:T(8,128)S(1)} fusion(f32[16,16,128]{2,1,0:T(8,128)} %bitcast.35, f32[18,18,130]{2,1,0:T(8,128)S(1)} %select_maximum_fusion.38, f32[1,16,128]{2,1,0:T(8,128)S(1)} %collective-permute-done.1, f32[1,16,128]{2,1,0:T(8,128)S(1)} %collective-permute-done, f32[16,16,128]{2,1,0:T(8,128)} %param.9, f32[]{:T(128)} %fusion.103, ...), kind=kLoop, calls=%fused_computation.263 | loop fusion | flops 1474560 | bytes 1065028 | tf_op jit(solution)/shard_map/add | solution.py:47
  25.9 3.9 collective-permute-start.2
  31.4 11.8 %fusion.96 = f32[16,16,128]{2,1,0:T(8,128)S(1)} fusion(f32[16,16,128]{2,1,0:T(8,128)S(1)} %fusion.101, f32[18,18,130]{2,1,0:T(8,128)S(1)} %select_maximum_fusion.36, f32[1,16,128]{2,1,0:T(8,128)S(1)} %collective-permute-done.3, f32[1,16,128]{2,1,0:T(8,128)S(1)} %collective-permute-done.2, f32[16,16,128]{2,1,0:T(8,128)} %param.9, f32[]{:T(128)} %fusion.103, ...), kind=kLoop, calls=%fused_computation.252 | loop fusion | flops 1474560 | bytes 1065028 | tf_op jit(solution)/shard_map/add | solution.py:47
  50.3 10.8 %fusion.91 = f32[16,16,128]{2,1,0:T(8,128)S(1)} fusion(f32[16,16,128]{2,1,0:T(8,128)S(1)} %fusion.96, f32[18,18,130]{2,1,0:T(8,128)S(1)} %select_maximum_fusion.34, f32[1,16,128]{2,1,0:T(8,128)S(1)} %collective-permute-done.5, f32[1,16,128]{2,1,0:T(8,128)S(1)} %collective-permute-done.4, f32[16,16,128]{2,1,0:T(8,128)S(1)} %copy-done, f32[]{:T(128)} %fusion.103, ...), kind=kLoop, calls=%fused_computation.241 | loop fusion | flops 1474560 | bytes 1065028 | tf_op jit(solution)/shard_map/add | solution.py:47
  61.1 4.1 collective-permute-start.7
  68.6 10.8 %fusion.86 = f32[16,16,128]{2,1,0:T(8,128)S(1)} fusion(f32[16,16,128]{2,1,0:T(8,128)S(1)} %fusion.91, f32[18,18,130]{2,1,0:T(8,128)S(1)} %select_maximum_fusion.32, f32[1,16,128]{2,1,0:T(8,128)S(1)} %collective-permute-done.7, f32[1,16,128]{2,1,0:T(8,128)S(1)} %collective-permute-done.6, f32[16,16,128]{2,1,0:T(8,128)S(1)} %copy-done, f32[]{:T(128)} %fusion.103, ...), kind=kLoop, calls=%fused_computation.230 | loop fusion | flops 1474560 | bytes 1065028 | tf_op jit(solution)/shard_map/add | solution.py:47
  79.5 3.6 collective-permute-start.9
  86.7 10.8 %fusion.81 = f32[16,16,128]{2,1,0:T(8,128)S(1)} fusion(f32[16,16,128]{2,1,0:T(8,128)S(1)} %fusion.86, f32[18,18,130]{2,1,0:T(8,128)S(1)} %select_maximum_fusion.30, f32[1,16,128]{2,1,0:T(8,128)S(1)} %collective-permute-done.9, f32[1,16,128]{2,1,0:T(8,128)S(1)} %collective-permute-done.8, f32[16,16,128]{2,1,0:T(8,128)S(1)} %copy-done, f32[]{:T(128)} %fusion.103, ...), kind=kLoop, calls=%fused_computation.219 | loop fusion | flops 1474560 | bytes 1065028 | tf_op jit(solution)/shard_map/add | solution.py:47
  97.5 3.6 collective-permute-start.11
  104.6 10.8 %fusion.76 = f32[16,16,128]{2,1,0:T(8,128)S(1)} fusion(f32[16,16,128]{2,1,0:T(8,128)S(1)} %fusion.81, f32[18,18,130]{2,1,0:T(8,128)S(1)} %select_maximum_fusion.28, f32[1,16,128]{2,1,0:T(8,128)S(1)} %collective-permute-done.11, f32[1,16,128]{2,1,0:T(8,128)S(1)} %collective-permute-done.10, f32[16,16,128]{2,1,0:T(8,128)S(1)} %copy-done, f32[]{:T(128)} %fusion.103, ...), kind=kLoop, calls=%fused_computation.208 | loop fusion | flops 1474560 | bytes 1065028 | tf_op jit(solution)/shard_map/add | solution.py:47
  115.5 3.6 collective-permute-start.13
  122.6 10.8 %fusion.71 = f32[16,16,128]{2,1,0:T(8,128)S(1)} fusion(f32[16,16,128]{2,1,0:T(8,128)S(1)} %fusion.76, f32[18,18,130]{2,1,0:T(8,128)S(1)} %select_maximum_fusion.26, f32[1,16,128]{2,1,0:T(8,128)S(1)} %collective-permute-done.13, f32[1,16,128]{2,1,0:T(8,128)S(1)} %collective-permute-done.12, f32[16,16,128]{2,1,0:T(8,128)S(1)} %copy-done, f32[]{:T(128)} %fusion.103, ...), kind=kLoop, calls=%fused_computation.197 | loop fusion | flops 1474560 | bytes 1065028 | tf_op jit(solution)/shard_map/add | solution.py:47
  133.4 3.6 collective-permute-start.15
  140.5 10.8 %fusion.66 = f32[16,16,128]{2,1,0:T(8,128)S(1)} fusion(f32[16,16,128]{2,1,0:T(8,128)S(1)} %fusion.71, f32[18,18,130]{2,1,0:T(8,128)S(1)} %select_maximum_fusion.24, f32[1,16,128]{2,1,0:T(8,128)S(1)} %collective-permute-done.15, f32[1,16,128]{2,1,0:T(8,128)S(1)} %collective-permute-done.14, f32[16,16,128]{2,1,0:T(8,128)S(1)} %copy-done, f32[]{:T(128)} %fusion.103, ...), kind=kLoop, calls=%fused_computation.186 | loop fusion | flops 1474560 | bytes 1065028 | tf_op jit(solution)/shard_map/add | solution.py:47
  151.3 3.6 collective-permute-start.17
  158.4 10.8 %fusion.61 = f32[16,16,128]{2,1,0:T(8,128)S(1)} fusion(f32[16,16,128]{2,1,0:T(8,128)S(1)} %fusion.66, f32[18,18,130]{2,1,0:T(8,128)S(1)} %select_maximum_fusion.22, f32[1,16,128]{2,1,0:T(8,128)S(1)} %collective-permute-done.17, f32[1,16,128]{2,1,0:T(8,128)S(1)} %collective-permute-done.16, f32[16,16,128]{2,1,0:T(8,128)S(1)} %copy-done, f32[]{:T(128)} %fusion.103, ...), kind=kLoop, calls=%fused_computation.175 | loop fusion | flops 1474560 | bytes 1065028 | tf_op jit(solution)/shard_map/add | solution.py:47
  169.2 3.6 collective-permute-start.19
  174.8 5.7 reshape_squeeze.3
  183.3 10.8 %fusion.56 = f32[16,16,128]{2,1,0:T(8,128)S(1)} fusion(f32[16,16,128]{2,1,0:T(8,128)S(1)} %fusion.61, f32[18,18,130]{2,1,0:T(8,128)S(1)} %select_maximum_fusion.20, f32[1,16,128]{2,1,0:T(8,128)S(1)} %collective-permute-done.19, f32[1,16,128]{2,1,0:T(8,128)S(1)} %collective-permute-done.18, f32[16,16,128]{2,1,0:T(8,128)S(1)} %copy-done, f32[]{:T(128)} %fusion.103, ...), kind=kLoop, calls=%fused_computation.164 | loop fusion | flops 1474560 | bytes 1065028 | tf_op jit(solution)/shard_map/add | solution.py:47
  194.2 5.7 reshape.37
  202.5 227.3 %all-gather = f32[256,4,32]{2,1,0:T(4,128)S(1)} all-gather(f32[4,4,32]{2,1,0:T(4,128)S(1)} %get-tuple-element.46), channel_id=2, replica_groups=mesh['tm'=64,'space'=8] {'tm'}, dimensions={0}, use_global_device_ids=true | all-gather | bytes 133120 | tf_op jit(solution)/shard_map/all_gather | solution.py:78
  432.7 4.9 reshape.38
  439.5 13.1 %collective-permute-done.20 = f32[16,16,128]{2,1,0:T(8,128)S(1)} collective-permute-done((f32[16,16,128]{2,1,0:T(8,128)S(1)}, f32[16,16,128]{2,1,0:T(8,128)S(1)}, u32[]{:S(2)}, u32[]{:S(2)}) %collective-permute-start.20) | collective-permute-done | bytes 131104 | tf_op jit(solution)/shard_map/ppermute | solution.py:26
  454.5 3.6 collective-permute-start.21
  459.7 10.8 %fusion.51 = f32[16,16,128]{2,1,0:T(8,128)S(1)} fusion(f32[16,16,128]{2,1,0:T(8,128)S(1)} %collective-permute-done.20, f32[18,18,130]{2,1,0:T(8,128)S(1)} %select_maximum_fusion.18, f32[1,16,128]{2,1,0:T(8,128)S(1)} %collective-permute-done.22, f32[1,16,128]{2,1,0:T(8,128)S(1)} %collective-permute-done.21, f32[16,16,128]{2,1,0:T(8,128)S(1)} %copy-done, ...), kind=kLoop, calls=%fused_computation.153 | loop fusion | flops 1474560 | bytes 1065028 | tf_op jit(solution)/shard_map/add | solution.py:47
  470.5 4.3 collective-permute-start.24
  478.2 10.8 %fusion.46 = f32[16,16,128]{2,1,0:T(8,128)S(1)} fusion(f32[16,16,128]{2,1,0:T(8,128)S(1)} %fusion.51, f32[18,18,130]{2,1,0:T(8,128)S(1)} %select_maximum_fusion.16, f32[1,16,128]{2,1,0:T(8,128)S(1)} %collective-permute-done.24, f32[1,16,128]{2,1,0:T(8,128)S(1)} %collective-permute-done.23, f32[16,16,128]{2,1,0:T(8,128)S(1)} %copy-done, f32[]{:T(128)} %fusion.103, ...), kind=kLoop, calls=%fused_computation.142 | loop fusion | flops 1474560 | bytes 1065028 | tf_op jit(solution)/shard_map/add | solution.py:47
  489.1 3.6 collective-permute-start.26
  496.2 10.8 %fusion.41 = f32[16,16,128]{2,1,0:T(8,128)S(1)} fusion(f32[16,16,128]{2,1,0:T(8,128)S(1)} %fusion.46, f32[18,18,130]{2,1,0:T(8,128)S(1)} %select_maximum_fusion.14, f32[1,16,128]{2,1,0:T(8,128)S(1)} %collective-permute-done.26, f32[1,16,128]{2,1,0:T(8,128)S(1)} %collective-permute-done.25, f32[16,16,128]{2,1,0:T(8,128)S(1)} %copy-done, f32[]{:T(128)} %fusion.103, ...), kind=kLoop, calls=%fused_computation.131 | loop fusion | flops 1474560 | bytes 1065028 | tf_op jit(solution)/shard_map/add | solution.py:47
  507.0 3.6 collective-permute-start.28
  514.1 10.8 %fusion.36 = f32[16,16,128]{2,1,0:T(8,128)S(1)} fusion(f32[16,16,128]{2,1,0:T(8,128)S(1)} %fusion.41, f32[18,18,130]{2,1,0:T(8,128)S(1)} %select_maximum_fusion.12, f32[1,16,128]{2,1,0:T(8,128)S(1)} %collective-permute-done.28, f32[1,16,128]{2,1,0:T(8,128)S(1)} %collective-permute-done.27, f32[16,16,128]{2,1,0:T(8,128)S(1)} %copy-done, f32[]{:T(128)} %fusion.103, ...), kind=kLoop, calls=%fused_computation.120 | loop fusion | flops 1474560 | bytes 1065028 | tf_op jit(solution)/shard_map/add | solution.py:47
  524.9 3.6 collective-permute-start.30
  532.0 10.8 %fusion.31 = f32[16,16,128]{2,1,0:T(8,128)S(1)} fusion(f32[16,16,128]{2,1,0:T(8,128)S(1)} %fusion.36, f32[18,18,130]{2,1,0:T(8,128)S(1)} %select_maximum_fusion.10, f32[1,16,128]{2,1,0:T(8,128)S(1)} %collective-permute-done.30, f32[1,16,128]{2,1,0:T(8,128)S(1)} %collective-permute-done.29, f32[16,16,128]{2,1,0:T(8,128)S(1)} %copy-done, f32[]{:T(128)} %fusion.103, ...), kind=kLoop, calls=%fused_computation.109 | loop fusion | flops 1474560 | bytes 1065028 | tf_op jit(solution)/shard_map/add | solution.py:47
  542.8 3.6 collective-permute-start.32
  549.9 10.8 %fusion.26 = f32[16,16,128]{2,1,0:T(8,128)S(1)} fusion(f32[16,16,128]{2,1,0:T(8,128)S(1)} %fusion.31, f32[18,18,130]{2,1,0:T(8,128)S(1)} %select_maximum_fusion.8, f32[1,16,128]{2,1,0:T(8,128)S(1)} %collective-permute-done.32, f32[1,16,128]{2,1,0:T(8,128)S(1)} %collective-permute-done.31, f32[16,16,128]{2,1,0:T(8,128)S(1)} %copy-done, f32[]{:T(128)} %fusion.103, ...), kind=kLoop, calls=%fused_computation.98 | loop fusion | flops 1474560 | bytes 1065028 | tf_op jit(solution)/shard_map/add | solution.py:47
  560.8 3.6 collective-permute-start.34
  567.9 10.8 %fusion.21 = f32[16,16,128]{2,1,0:T(8,128)S(1)} fusion(f32[16,16,128]{2,1,0:T(8,128)S(1)} %fusion.26, f32[18,18,130]{2,1,0:T(8,128)S(1)} %select_maximum_fusion.6, f32[1,16,128]{2,1,0:T(8,128)S(1)} %collective-permute-done.34, f32[1,16,128]{2,1,0:T(8,128)S(1)} %collective-permute-done.33, f32[16,16,128]{2,1,0:T(8,128)S(1)} %copy-done, f32[]{:T(128)} %fusion.103, ...), kind=kLoop, calls=%fused_computation.87 | loop fusion | flops 1474560 | bytes 1065028 | tf_op jit(solution)/shard_map/add | solution.py:47
  578.7 3.6 collective-permute-start.36
  585.8 10.8 %fusion.16 = f32[16,16,128]{2,1,0:T(8,128)S(1)} fusion(f32[16,16,128]{2,1,0:T(8,128)S(1)} %fusion.21, f32[18,18,130]{2,1,0:T(8,128)S(1)} %select_maximum_fusion.4, f32[1,16,128]{2,1,0:T(8,128)S(1)} %collective-permute-done.36, f32[1,16,128]{2,1,0:T(8,128)S(1)} %collective-permute-done.35, f32[16,16,128]{2,1,0:T(8,128)S(1)} %copy-done, f32[]{:T(128)} %fusion.103, ...), kind=kLoop, calls=%fused_computation.76 | loop fusion | flops 1474560 | bytes 1065028 | tf_op jit(solution)/shard_map/add | solution.py:47
  603.7 10.8 %fusion.11 = f32[16,16,128]{2,1,0:T(8,128)S(1)} fusion(f32[16,16,128]{2,1,0:T(8,128)S(1)} %fusion.16, f32[18,18,130]{2,1,0:T(8,128)S(1)} %select_maximum_fusion.2, f32[1,16,128]{2,1,0:T(8,128)S(1)} %collective-permute-done.38, f32[1,16,128]{2,1,0:T(8,128)S(1)} %collective-permute-done.37, f32[16,16,128]{2,1,0:T(8,128)S(1)} %copy-done, f32[]{:T(128)} %fusion.103, ...), kind=kLoop, calls=%fused_computation.65 | loop fusion | flops 1474560 | bytes 1065028 | tf_op jit(solution)/shard_map/add | solution.py:47
  614.5 3.6 collective-permute-start.40
  620.3 5.7 reshape.40
  628.8 10.8 %fusion.6 = f32[16,16,128]{2,1,0:T(8,128)S(1)} fusion(f32[16,16,128]{2,1,0:T(8,128)S(1)} %fusion.11, f32[18,18,130]{2,1,0:T(8,128)S(1)} %select_maximum_fusion, f32[1,16,128]{2,1,0:T(8,128)S(1)} %collective-permute-done.40, f32[1,16,128]{2,1,0:T(8,128)S(1)} %collective-permute-done.39, f32[16,16,128]{2,1,0:T(8,128)S(1)} %copy-done, f32[]{:T(128)} %fusion.103, ...), kind=kLoop, calls=%fused_computation.54 | loop fusion | flops 1474560 | bytes 1065028 | tf_op jit(solution)/shard_map/add | solution.py:47
  639.6 5.7 reshape.39
  647.9 215.9 %all-gather.1 = f32[256,4,32]{2,1,0:T(4,128)S(1)} all-gather(f32[4,4,32]{2,1,0:T(4,128)S(1)} %multiply_subtract_fusion), channel_id=3, replica_groups=mesh['tm'=64,'space'=8] {'tm'}, dimensions={0}, use_global_device_ids=true | all-gather | bytes 133120 | tf_op jit(solution)/shard_map/all_gather | solution.py:78
  866.8 4.9 reshape.41
  874.9 11.8 %collective-permute-done.41 = f32[16,16,128]{2,1,0:T(8,128)S(1)} collective-permute-done((f32[16,16,128]{2,1,0:T(8,128)S(1)}, f32[16,16,128]{2,1,0:T(8,128)S(1)}, u32[]{:S(2)}, u32[]{:S(2)}) %collective-permute-start.41) | collective-permute-done | bytes 131104 | tf_op jit(solution)/shard_map/ppermute | solution.py:26
  (130 shorter events, 100.2 us)
Async XLA Ops:
  0.0 50.3 %copy-start = (f32[16,16,128]{2,1,0:T(8,128)S(1)}, f32[16,16,128]{2,1,0:T(8,128)}, u32[]{:S(2)}) copy-start(f32[16,16,128]{2,1,0:T(8,128)} %param.9) | copy-start | bytes 393220
  0.0 50.3 %copy-start.1 = (s32[16,16,128]{2,1,0:T(8,128)S(1)}, s32[16,16,128]{2,1,0:T(8,128)}, u32[]{:S(2)}) copy-start(s32[16,16,128]{2,1,0:T(8,128)} %param.8) | copy-start | bytes 393220
  0.8 9.4 %collective-permute-start.1 = (f32[1,16,128]{2,1,0:T(8,128)S(1)}, f32[1,16,128]{2,1,0:T(8,128)S(1)}, u32[]{:S(2)}, u32[]{:S(2)}) collective-permute-start(f32[1,16,128]{2,1,0:T(8,128)S(1)} %get-tuple-element.43), channel_id=1, source_target_pairs={{0,1},{1,2},{2,3},{3,4},{4,5},{5,6},{6,7},{8,9},{9,10},{10,11},{11... | collective-permute-start | bytes 24584 | tf_op jit(solution)/shard_map/ppermute | solution.py:15
  2.7 7.5 collective-permute-start
  23.3 6.6 collective-permute-start.3
  25.9 5.3 collective-permute-start.2
  43.2 5.6 collective-permute-start.5
  46.5 3.6 collective-permute-start.4
  61.1 6.0 collective-permute-start.7
  65.2 3.3 collective-permute-start.6
  79.5 5.7 collective-permute-start.9
  83.1 91.7 %copy-start.2 = (f32[1,16,16,128]{3,2,1,0:T(8,128)S(1)}, f32[1,16,16,128]{3,2,1,0:T(8,128)}, u32[]{:S(2)}) copy-start(f32[1,16,16,128]{3,2,1,0:T(8,128)} %param.7) | copy-start | bytes 393220
  83.1 3.4 collective-permute-start.8
  97.5 5.6 collective-permute-start.11
  101.2 3.3 collective-permute-start.10
  115.5 5.6 collective-permute-start.13
  119.1 3.3 collective-permute-start.12
  133.4 5.6 collective-permute-start.15
  137.0 3.3 collective-permute-start.14
  151.3 5.6 collective-permute-start.17
  155.0 3.3 collective-permute-start.16
  169.2 13.9 %collective-permute-start.19 = (f32[1,16,128]{2,1,0:T(8,128)S(1)}, f32[1,16,128]{2,1,0:T(8,128)S(1)}, u32[]{:S(2)}, u32[]{:S(2)}) collective-permute-start(f32[1,16,128]{2,1,0:T(8,128)S(1)} %get-tuple-element.25), channel_id=1, source_target_pairs={{0,1},{1,2},{2,3},{3,4},{4,5},{5,6},{6,7},{8,9},{9,10},{10,11},{11... | collective-permute-start | bytes 24584 | tf_op jit(solution)/shard_map/ppermute | solution.py:15
  172.9 10.3 %collective-permute-start.18 = (f32[1,16,128]{2,1,0:T(8,128)S(1)}, f32[1,16,128]{2,1,0:T(8,128)S(1)}, u32[]{:S(2)}, u32[]{:S(2)}) collective-permute-start(f32[1,16,128]{2,1,0:T(8,128)S(1)} %get-tuple-element.26), channel_id=1, source_target_pairs={{1,0},{2,1},{3,2},{4,3},{5,4},{6,5},{7,6},{9,8},{10,9},{11,10},{12... | collective-permute-start | bytes 24584 | tf_op jit(solution)/shard_map/ppermute | solution.py:18
  194.1 8.3 copy-start.3
  437.6 15.0 %collective-permute-start.20 = (f32[16,16,128]{2,1,0:T(8,128)S(1)}, f32[16,16,128]{2,1,0:T(8,128)S(1)}, u32[]{:S(2)}, u32[]{:S(2)}) collective-permute-start(f32[16,16,128]{2,1,0:T(8,128)S(1)} %add.550), channel_id=1, source_target_pairs={{504,0},{0,8},{8,16},{16,24},{24,32},{32,40},{40,48},{48,56},{56,6... | collective-permute-start | bytes 393224 | tf_op jit(solution)/shard_map/ppermute | solution.py:26
  452.6 5.6 collective-permute-start.22
  454.5 5.0 collective-permute-start.21
  470.5 6.2 collective-permute-start.24
  474.8 3.3 collective-permute-start.23
  489.1 5.6 collective-permute-start.26
  492.7 3.3 collective-permute-start.25
  507.0 5.6 collective-permute-start.28
  510.6 3.3 collective-permute-start.27
  524.9 5.6 collective-permute-start.30
  528.6 3.3 collective-permute-start.29
  542.8 5.6 collective-permute-start.32
  546.5 3.3 collective-permute-start.31
  560.8 5.6 collective-permute-start.34
  564.4 3.3 collective-permute-start.33
  578.7 5.6 collective-permute-start.36
  582.3 3.3 collective-permute-start.35
  596.6 5.6 collective-permute-start.38
  600.2 3.3 collective-permute-start.37
  614.5 14.1 %collective-permute-start.40 = (f32[1,16,128]{2,1,0:T(8,128)S(1)}, f32[1,16,128]{2,1,0:T(8,128)S(1)}, u32[]{:S(2)}, u32[]{:S(2)}) collective-permute-start(f32[1,16,128]{2,1,0:T(8,128)S(1)} %get-tuple-element.5), channel_id=1, source_target_pairs={{0,1},{1,2},{2,3},{3,4},{4,5},{5,6},{6,7},{8,9},{9,10},{10,11},{11... | collective-permute-start | bytes 24584 | tf_op jit(solution)/shard_map/ppermute | solution.py:15
  618.2 10.5 %collective-permute-start.39 = (f32[1,16,128]{2,1,0:T(8,128)S(1)}, f32[1,16,128]{2,1,0:T(8,128)S(1)}, u32[]{:S(2)}, u32[]{:S(2)}) collective-permute-start(f32[1,16,128]{2,1,0:T(8,128)S(1)} %get-tuple-element.6), channel_id=1, source_target_pairs={{1,0},{2,1},{3,2},{4,3},{5,4},{6,5},{7,6},{9,8},{10,9},{11,10},{12... | collective-permute-start | bytes 24584 | tf_op jit(solution)/shard_map/ppermute | solution.py:18
  871.7 15.0 %collective-permute-start.41 = (f32[16,16,128]{2,1,0:T(8,128)S(1)}, f32[16,16,128]{2,1,0:T(8,128)S(1)}, u32[]{:S(2)}, u32[]{:S(2)}) collective-permute-start(f32[16,16,128]{2,1,0:T(8,128)S(1)} %add.621), channel_id=1, source_target_pairs={{504,0},{0,8},{8,16},{16,24},{24,32},{32,40},{40,48},{48,56},{56,6... | collective-permute-start | bytes 393224 | tf_op jit(solution)/shard_map/ppermute | solution.py:26
where the time goes:
time: 892 us; the launch traced here: 887 us
  blocking collectives  443 us (50%)
  other arithmetic  235 us (26%)
  starting transfers between devices  119 us (13%)
  waiting for transfers between devices  47.6 us (5%)
  local copies, waits for them, and re-layouts  41.1 us (5%)
    all_gather x2, blocking collectives, body(): pieces = lax.all_gather(jump_now[None], 'tm', axis=0, tiled=True)  443 us
    add x20, other arithmetic, slab_update(): return field_now + cell_coef * (neighbours - 6.0 * field_now) + forcing  218 us
    ppermute x20, starting transfers between devices, padded_2(): lax.ppermute(lax.slice_in_dim(block, block.shape[dim] - width, None, axis...  69.2 us
    ppermute x20, starting transfers between devices, padded_2(): lax.ppermute(lax.slice_in_dim(block, 0, width, axis=dim), axis, backward)  44.5 us
    ppermute x2, waiting for transfers between devices, from_behind(): return lax.ppermute(block, axis, route)  24.9 us
    ppermute x20, waiting for transfers between devices, padded_2(): lax.ppermute(lax.slice_in_dim(block, 0, width, axis=dim), axis, backward)  22.7 us
  transfers between devices with their start and end apart: 42, of which 19 were waited for; matrix products, arithmetic and copies ran while one was open for 2% of the time, Pallas kernels for 0%

commit v1 on v0

--- a/solution.py
+++ b/solution.py
@@ -5,6 +5,13 @@
 
 FINE = 10
 ITERS = 2
+
+
+def swapped_in(x, axis, dim):
+    size = lax.axis_size(axis)
+    parts = jnp.stack([x for _ in range(size)])
+    parts = lax.all_to_all(parts, axis, split_axis=0, concat_axis=0)
+    return jnp.concatenate(parts, axis=dim)
 
 
 def padded_2(block, sides, width):
@@ -75,7 +82,7 @@
             finish = slab_update(finish, cell_coef, forcing)
         coarse_start = restrict(field_now)
         jump_now = restrict(finish) - decay * coarse_start
-        pieces = lax.all_gather(jump_now[None], "tm", axis=0, tiled=True)
+        pieces = swapped_in(jump_now[None], "tm", 0)
         count = pieces.shape[0]
         seen = jnp.arange(count, dtype=jnp.int32)
         lagged = (device_index - 1 - seen) % windows

time: 892 us -> 508 us (0.57)
  the two profiles are of different devices: /device:TPU:64 before, /device:TPU:1 now
where the time goes in v1:
time: 508 us; the launch traced here: 503 us
  other arithmetic  236 us (46%)
  starting transfers between devices  116 us (23%)
  waiting for transfers between devices  86.2 us (17%)
  local copies, waits for them, and re-layouts  43.5 us (9%)
  blocking collectives  18.8 us (4%)
    add x20, other arithmetic, slab_update(): return field_now + cell_coef * (neighbours - 6.0 * field_now) + forcing  217 us
    ppermute x20, starting transfers between devices, padded_2(): lax.ppermute(lax.slice_in_dim(block, 0, width, axis=dim), axis, backward)  49.5 us
    ppermute x20, waiting for transfers between devices, padded_2(): lax.ppermute(lax.slice_in_dim(block, 0, width, axis=dim), axis, backward)  45.5 us
    ppermute x20, starting transfers between devices, padded_2(): lax.ppermute(lax.slice_in_dim(block, block.shape[dim] - width, None, axis...  45 us
    ppermute x2, waiting for transfers between devices, from_behind(): return lax.ppermute(block, axis, route)  26 us
    all_to_all x1, blocking collectives, swapped_in(): parts = lax.all_to_all(parts, axis, split_axis=0, concat_axis=0)  18.8 us
    reshape x3, local copies, waits for them, and re-layouts, restrict(): blocks = field_now.reshape((depth // 4, 4, rows // 4, 4, cols // 4, 4))  17 us
    all_to_all x1, starting transfers between devices, swapped_in(): parts = lax.all_to_all(parts, axis, split_axis=0, concat_axis=0)  16.6 us
  transfers between devices with their start and end apart: 43, of which 20 were waited for; matrix products, arithmetic and copies ran while one was open for 4% of the time, Pallas kernels for 0%

profile of v1, /device:TPU:1, one launch (start us, length us, event | category | flops | bytes accessed | tf_op | source)
XLA Modules:
  0.0 503.0 jit_solution(428362355162330608)
XLA Ops:
  0.8 5.4 %collective-permute-start.1 = (f32[1,16,128]{2,1,0:T(8,128)S(1)}, f32[1,16,128]{2,1,0:T(8,128)S(1)}, u32[]{:S(2)}, u32[]{:S(2)}) collective-permute-start(f32[1,16,128]{2,1,0:T(8,128)S(1)} %get-tuple-element.43), channel_id=1, source_target_pairs={{0,1},{1,2},{2,3},{3,4},{4,5},{5,6},{6,7},{8,9},{9,10},{10,11},{11... | collective-permute-start | bytes 24584 | tf_op jit(solution)/shard_map/ppermute | solution.py:22
  6.1 4.7 collective-permute-start
  15.7 11.9 %fusion.103 = f32[16,16,128]{2,1,0:T(8,128)S(1)} fusion(f32[16,16,128]{2,1,0:T(8,128)} %bitcast.39, f32[18,18,130]{2,1,0:T(8,128)S(1)} %select_maximum_fusion.38, f32[1,16,128]{2,1,0:T(8,128)S(1)} %collective-permute-done.1, f32[1,16,128]{2,1,0:T(8,128)S(1)} %collective-permute-done, f32[16,16,128]{2,1,0:T(8,128)} %param.9, f32[]{:T(128)} %fusion.105, ...), kind=kLoop, calls=%fused_computation.265 | loop fusion | flops 1474560 | bytes 1065028 | tf_op jit(solution)/shard_map/add | solution.py:54
  34.8 11.7 %fusion.98 = f32[16,16,128]{2,1,0:T(8,128)S(1)} fusion(f32[16,16,128]{2,1,0:T(8,128)S(1)} %fusion.103, f32[18,18,130]{2,1,0:T(8,128)S(1)} %select_maximum_fusion.36, f32[1,16,128]{2,1,0:T(8,128)S(1)} %collective-permute-done.3, f32[1,16,128]{2,1,0:T(8,128)S(1)} %collective-permute-done.2, f32[16,16,128]{2,1,0:T(8,128)} %param.9, f32[]{:T(128)} %fusion.105, ...), kind=kLoop, calls=%fused_computation.254 | loop fusion | flops 1474560 | bytes 1065028 | tf_op jit(solution)/shard_map/add | solution.py:54
  53.6 10.8 %fusion.93 = f32[16,16,128]{2,1,0:T(8,128)S(1)} fusion(f32[16,16,128]{2,1,0:T(8,128)S(1)} %fusion.98, f32[18,18,130]{2,1,0:T(8,128)S(1)} %select_maximum_fusion.34, f32[1,16,128]{2,1,0:T(8,128)S(1)} %collective-permute-done.5, f32[1,16,128]{2,1,0:T(8,128)S(1)} %collective-permute-done.4, f32[16,16,128]{2,1,0:T(8,128)S(1)} %copy-done, f32[]{:T(128)} %fusion.105, ...), kind=kLoop, calls=%fused_computation.243 | loop fusion | flops 1474560 | bytes 1065028 | tf_op jit(solution)/shard_map/add | solution.py:54
  68.8 3.0 collective-permute-done.6
  71.9 10.8 %fusion.88 = f32[16,16,128]{2,1,0:T(8,128)S(1)} fusion(f32[16,16,128]{2,1,0:T(8,128)S(1)} %fusion.93, f32[18,18,130]{2,1,0:T(8,128)S(1)} %select_maximum_fusion.32, f32[1,16,128]{2,1,0:T(8,128)S(1)} %collective-permute-done.7, f32[1,16,128]{2,1,0:T(8,128)S(1)} %collective-permute-done.6, f32[16,16,128]{2,1,0:T(8,128)S(1)} %copy-done, f32[]{:T(128)} %fusion.105, ...), kind=kLoop, calls=%fused_computation.232 | loop fusion | flops 1474560 | bytes 1065028 | tf_op jit(solution)/shard_map/add | solution.py:54
  90.0 10.8 %fusion.83 = f32[16,16,128]{2,1,0:T(8,128)S(1)} fusion(f32[16,16,128]{2,1,0:T(8,128)S(1)} %fusion.88, f32[18,18,130]{2,1,0:T(8,128)S(1)} %select_maximum_fusion.30, f32[1,16,128]{2,1,0:T(8,128)S(1)} %collective-permute-done.9, f32[1,16,128]{2,1,0:T(8,128)S(1)} %collective-permute-done.8, f32[16,16,128]{2,1,0:T(8,128)S(1)} %copy-done, f32[]{:T(128)} %fusion.105, ...), kind=kLoop, calls=%fused_computation.221 | loop fusion | flops 1474560 | bytes 1065028 | tf_op jit(solution)/shard_map/add | solution.py:54
  107.9 10.8 %fusion.78 = f32[16,16,128]{2,1,0:T(8,128)S(1)} fusion(f32[16,16,128]{2,1,0:T(8,128)S(1)} %fusion.83, f32[18,18,130]{2,1,0:T(8,128)S(1)} %select_maximum_fusion.28, f32[1,16,128]{2,1,0:T(8,128)S(1)} %collective-permute-done.11, f32[1,16,128]{2,1,0:T(8,128)S(1)} %collective-permute-done.10, f32[16,16,128]{2,1,0:T(8,128)S(1)} %copy-done, f32[]{:T(128)} %fusion.105, ...), kind=kLoop, calls=%fused_computation.210 | loop fusion | flops 1474560 | bytes 1065028 | tf_op jit(solution)/shard_map/add | solution.py:54
  125.8 10.8 %fusion.73 = f32[16,16,128]{2,1,0:T(8,128)S(1)} fusion(f32[16,16,128]{2,1,0:T(8,128)S(1)} %fusion.78, f32[18,18,130]{2,1,0:T(8,128)S(1)} %select_maximum_fusion.26, f32[1,16,128]{2,1,0:T(8,128)S(1)} %collective-permute-done.13, f32[1,16,128]{2,1,0:T(8,128)S(1)} %collective-permute-done.12, f32[16,16,128]{2,1,0:T(8,128)S(1)} %copy-done, f32[]{:T(128)} %fusion.105, ...), kind=kLoop, calls=%fused_computation.199 | loop fusion | flops 1474560 | bytes 1065028 | tf_op jit(solution)/shard_map/add | solution.py:54
  143.6 10.8 %fusion.68 = f32[16,16,128]{2,1,0:T(8,128)S(1)} fusion(f32[16,16,128]{2,1,0:T(8,128)S(1)} %fusion.73, f32[18,18,130]{2,1,0:T(8,128)S(1)} %select_maximum_fusion.24, f32[1,16,128]{2,1,0:T(8,128)S(1)} %collective-permute-done.15, f32[1,16,128]{2,1,0:T(8,128)S(1)} %collective-permute-done.14, f32[16,16,128]{2,1,0:T(8,128)S(1)} %copy-done, f32[]{:T(128)} %fusion.105, ...), kind=kLoop, calls=%fused_computation.188 | loop fusion | flops 1474560 | bytes 1065028 | tf_op jit(solution)/shard_map/add | solution.py:54
  158.8 2.6 collective-permute-done.16
  161.5 10.8 %fusion.63 = f32[16,16,128]{2,1,0:T(8,128)S(1)} fusion(f32[16,16,128]{2,1,0:T(8,128)S(1)} %fusion.68, f32[18,18,130]{2,1,0:T(8,128)S(1)} %select_maximum_fusion.22, f32[1,16,128]{2,1,0:T(8,128)S(1)} %collective-permute-done.17, f32[1,16,128]{2,1,0:T(8,128)S(1)} %collective-permute-done.16, f32[16,16,128]{2,1,0:T(8,128)S(1)} %copy-done, f32[]{:T(128)} %fusion.105, ...), kind=kLoop, calls=%fused_computation.177 | loop fusion | flops 1474560 | bytes 1065028 | tf_op jit(solution)/shard_map/add | solution.py:54
  176.7 5.7 %reshape_squeeze.3 = f32[4,4,4,4,32,4]{5,4,3,2,1,0:T(8,128)} reshape(f32[1,16,16,128]{3,2,1,0:T(8,128)S(1)} %copy-done.2) | data formatting | bytes 262144 | tf_op jit(solution)/shard_map/reshape;squeeze | solution.py:59
  182.3 2.6 reduce_sum.69
  185.2 10.8 %fusion.58 = f32[16,16,128]{2,1,0:T(8,128)S(1)} fusion(f32[16,16,128]{2,1,0:T(8,128)S(1)} %fusion.63, f32[18,18,130]{2,1,0:T(8,128)S(1)} %select_maximum_fusion.20, f32[1,16,128]{2,1,0:T(8,128)S(1)} %collective-permute-done.19, f32[1,16,128]{2,1,0:T(8,128)S(1)} %collective-permute-done.18, f32[16,16,128]{2,1,0:T(8,128)S(1)} %copy-done, f32[]{:T(128)} %fusion.105, ...), kind=kLoop, calls=%fused_computation.166 | loop fusion | flops 1474560 | bytes 1065028 | tf_op jit(solution)/shard_map/add | solution.py:54
  195.9 5.7 %reshape.47 = f32[4,4,4,4,32,4]{5,4,3,2,1,0:T(8,128)} reshape(f32[16,16,128]{2,1,0:T(8,128)S(1)} %fusion.58) | data formatting | bytes 262144 | tf_op jit(solution)/shard_map/reshape | solution.py:59
  201.6 2.6 reduce_sum.68
  205.3 16.6 %all-to-all-start = ((f32[64,1,512]{2,1,0:T(1,128)}), f32[64,1,512]{2,1,0:T(1,128)S(1)}, u32[]{:S(2)}, u32[]{:S(2)}) async-start(f32[64,1,512]{2,1,0:T(1,128)} %reshape.54), calls=%async_computation | async-start | bytes 262144 | tf_op jit(solution)/shard_map/all_to_all | solution.py:13
  221.9 14.6 %all-to-all-done = f32[64,1,512]{2,1,0:T(1,128)S(1)} async-done(((f32[64,1,512]{2,1,0:T(1,128)}), f32[64,1,512]{2,1,0:T(1,128)S(1)}, u32[]{:S(2)}, u32[]{:S(2)}) %all-to-all-start) | async-done | bytes 131104 | tf_op jit(solution)/shard_map/all_to_all | solution.py:13
  238.7 2.6 broadcast_in_dim.94
  241.2 4.9 reshape.49
  246.1 2.9 collective-permute-start.20
  249.0 12.3 %collective-permute-done.20 = f32[16,16,128]{2,1,0:T(8,128)S(1)} collective-permute-done((f32[16,16,128]{2,1,0:T(8,128)S(1)}, f32[16,16,128]{2,1,0:T(8,128)S(1)}, u32[]{:S(2)}, u32[]{:S(2)}) %collective-permute-start.20) | collective-permute-done | bytes 131104 | tf_op jit(solution)/shard_map/ppermute | solution.py:33
  261.2 4.4 collective-permute-start.22
  267.6 3.0 collective-permute-done.21
  270.8 10.8 %fusion.53 = f32[16,16,128]{2,1,0:T(8,128)S(1)} fusion(f32[16,16,128]{2,1,0:T(8,128)S(1)} %collective-permute-done.20, f32[18,18,130]{2,1,0:T(8,128)S(1)} %select_maximum_fusion.18, f32[1,16,128]{2,1,0:T(8,128)S(1)} %collective-permute-done.22, f32[1,16,128]{2,1,0:T(8,128)S(1)} %collective-permute-done.21, f32[16,16,128]{2,1,0:T(8,128)S(1)} %copy-done, ...), kind=kLoop, calls=%fused_computation.155 | loop fusion | flops 1474560 | bytes 1065028 | tf_op jit(solution)/shard_map/add | solution.py:54
  285.9 3.5 collective-permute-done.23
  289.6 10.8 %fusion.48 = f32[16,16,128]{2,1,0:T(8,128)S(1)} fusion(f32[16,16,128]{2,1,0:T(8,128)S(1)} %fusion.53, f32[18,18,130]{2,1,0:T(8,128)S(1)} %select_maximum_fusion.16, f32[1,16,128]{2,1,0:T(8,128)S(1)} %collective-permute-done.24, f32[1,16,128]{2,1,0:T(8,128)S(1)} %collective-permute-done.23, f32[16,16,128]{2,1,0:T(8,128)S(1)} %copy-done, f32[]{:T(128)} %fusion.105, ...), kind=kLoop, calls=%fused_computation.144 | loop fusion | flops 1474560 | bytes 1065028 | tf_op jit(solution)/shard_map/add | solution.py:54
  304.7 2.6 collective-permute-done.25
  307.5 10.8 %fusion.43 = f32[16,16,128]{2,1,0:T(8,128)S(1)} fusion(f32[16,16,128]{2,1,0:T(8,128)S(1)} %fusion.48, f32[18,18,130]{2,1,0:T(8,128)S(1)} %select_maximum_fusion.14, f32[1,16,128]{2,1,0:T(8,128)S(1)} %collective-permute-done.26, f32[1,16,128]{2,1,0:T(8,128)S(1)} %collective-permute-done.25, f32[16,16,128]{2,1,0:T(8,128)S(1)} %copy-done, f32[]{:T(128)} %fusion.105, ...), kind=kLoop, calls=%fused_computation.133 | loop fusion | flops 1474560 | bytes 1065028 | tf_op jit(solution)/shard_map/add | solution.py:54
  325.4 10.8 %fusion.38 = f32[16,16,128]{2,1,0:T(8,128)S(1)} fusion(f32[16,16,128]{2,1,0:T(8,128)S(1)} %fusion.43, f32[18,18,130]{2,1,0:T(8,128)S(1)} %select_maximum_fusion.12, f32[1,16,128]{2,1,0:T(8,128)S(1)} %collective-permute-done.28, f32[1,16,128]{2,1,0:T(8,128)S(1)} %collective-permute-done.27, f32[16,16,128]{2,1,0:T(8,128)S(1)} %copy-done, f32[]{:T(128)} %fusion.105, ...), kind=kLoop, calls=%fused_computation.122 | loop fusion | flops 1474560 | bytes 1065028 | tf_op jit(solution)/shard_map/add | solution.py:54
  343.3 10.8 %fusion.33 = f32[16,16,128]{2,1,0:T(8,128)S(1)} fusion(f32[16,16,128]{2,1,0:T(8,128)S(1)} %fusion.38, f32[18,18,130]{2,1,0:T(8,128)S(1)} %select_maximum_fusion.10, f32[1,16,128]{2,1,0:T(8,128)S(1)} %collective-permute-done.30, f32[1,16,128]{2,1,0:T(8,128)S(1)} %collective-permute-done.29, f32[16,16,128]{2,1,0:T(8,128)S(1)} %copy-done, f32[]{:T(128)} %fusion.105, ...), kind=kLoop, calls=%fused_computation.111 | loop fusion | flops 1474560 | bytes 1065028 | tf_op jit(solution)/shard_map/add | solution.py:54
  361.1 10.8 %fusion.28 = f32[16,16,128]{2,1,0:T(8,128)S(1)} fusion(f32[16,16,128]{2,1,0:T(8,128)S(1)} %fusion.33, f32[18,18,130]{2,1,0:T(8,128)S(1)} %select_maximum_fusion.8, f32[1,16,128]{2,1,0:T(8,128)S(1)} %collective-permute-done.32, f32[1,16,128]{2,1,0:T(8,128)S(1)} %collective-permute-done.31, f32[16,16,128]{2,1,0:T(8,128)S(1)} %copy-done, f32[]{:T(128)} %fusion.105, ...), kind=kLoop, calls=%fused_computation.100 | loop fusion | flops 1474560 | bytes 1065028 | tf_op jit(solution)/shard_map/add | solution.py:54
  379.0 10.8 %fusion.23 = f32[16,16,128]{2,1,0:T(8,128)S(1)} fusion(f32[16,16,128]{2,1,0:T(8,128)S(1)} %fusion.28, f32[18,18,130]{2,1,0:T(8,128)S(1)} %select_maximum_fusion.6, f32[1,16,128]{2,1,0:T(8,128)S(1)} %collective-permute-done.34, f32[1,16,128]{2,1,0:T(8,128)S(1)} %collective-permute-done.33, f32[16,16,128]{2,1,0:T(8,128)S(1)} %copy-done, f32[]{:T(128)} %fusion.105, ...), kind=kLoop, calls=%fused_computation.89 | loop fusion | flops 1474560 | bytes 1065028 | tf_op jit(solution)/shard_map/add | solution.py:54
  396.9 10.8 %fusion.18 = f32[16,16,128]{2,1,0:T(8,128)S(1)} fusion(f32[16,16,128]{2,1,0:T(8,128)S(1)} %fusion.23, f32[18,18,130]{2,1,0:T(8,128)S(1)} %select_maximum_fusion.4, f32[1,16,128]{2,1,0:T(8,128)S(1)} %collective-permute-done.36, f32[1,16,128]{2,1,0:T(8,128)S(1)} %collective-permute-done.35, f32[16,16,128]{2,1,0:T(8,128)S(1)} %copy-done, f32[]{:T(128)} %fusion.105, ...), kind=kLoop, calls=%fused_computation.78 | loop fusion | flops 1474560 | bytes 1065028 | tf_op jit(solution)/shard_map/add | solution.py:54
  414.8 10.8 %fusion.13 = f32[16,16,128]{2,1,0:T(8,128)S(1)} fusion(f32[16,16,128]{2,1,0:T(8,128)S(1)} %fusion.18, f32[18,18,130]{2,1,0:T(8,128)S(1)} %select_maximum_fusion.2, f32[1,16,128]{2,1,0:T(8,128)S(1)} %collective-permute-done.38, f32[1,16,128]{2,1,0:T(8,128)S(1)} %collective-permute-done.37, f32[16,16,128]{2,1,0:T(8,128)S(1)} %copy-done, f32[]{:T(128)} %fusion.105, ...), kind=kLoop, calls=%fused_computation.67 | loop fusion | flops 1474560 | bytes 1065028 | tf_op jit(solution)/shard_map/add | solution.py:54
  427.6 2.6 collective-permute-start.39
  430.2 5.7 %reshape.51 = f32[4,4,4,4,32,4]{5,4,3,2,1,0:T(8,128)} reshape(f32[16,16,128]{2,1,0:T(8,128)S(1)} %collective-permute-done.20) | data formatting | bytes 262144 | tf_op jit(solution)/shard_map/reshape | solution.py:59
  435.8 2.6 reduce_sum.72
  438.6 10.8 %fusion.8 = f32[16,16,128]{2,1,0:T(8,128)S(1)} fusion(f32[16,16,128]{2,1,0:T(8,128)S(1)} %fusion.13, f32[18,18,130]{2,1,0:T(8,128)S(1)} %select_maximum_fusion, f32[1,16,128]{2,1,0:T(8,128)S(1)} %collective-permute-done.40, f32[1,16,128]{2,1,0:T(8,128)S(1)} %collective-permute-done.39, f32[16,16,128]{2,1,0:T(8,128)S(1)} %copy-done, f32[]{:T(128)} %fusion.105, ...), kind=kLoop, calls=%fused_computation.56 | loop fusion | flops 1474560 | bytes 1065028 | tf_op jit(solution)/shard_map/add | solution.py:54
  449.4 5.7 %reshape.50 = f32[4,4,4,4,32,4]{5,4,3,2,1,0:T(8,128)} reshape(f32[16,16,128]{2,1,0:T(8,128)S(1)} %fusion.8) | data formatting | bytes 262144 | tf_op jit(solution)/shard_map/reshape | solution.py:59
  455.1 2.6 reduce_sum.71
  458.2 18.8 %all_to_all.10 = f32[64,1,512]{2,1,0:T(1,128)S(1)} all-to-all(f32[64,1,512]{2,1,0:T(1,128)S(1)} %reshape.56), channel_id=1, replica_groups=mesh['tm'=64,'space'=8] {'tm'}, dimensions={0} | all-to-all | bytes 262144 | tf_op jit(solution)/shard_map/all_to_all | solution.py:13
  478.6 2.6 broadcast_in_dim.95
  481.2 4.9 reshape.53
  486.0 2.6 collective-permute-start.41
  488.6 13.7 %collective-permute-done.41 = f32[16,16,128]{2,1,0:T(8,128)S(1)} collective-permute-done((f32[16,16,128]{2,1,0:T(8,128)S(1)}, f32[16,16,128]{2,1,0:T(8,128)S(1)}, u32[]{:S(2)}, u32[]{:S(2)}) %collective-permute-start.41) | collective-permute-done | bytes 131104 | tf_op jit(solution)/shard_map/ppermute | solution.py:33
  (140 shorter events, 122.8 us)
Async XLA Ops:
  0.0 53.6 %copy-start = (f32[16,16,128]{2,1,0:T(8,128)S(1)}, f32[16,16,128]{2,1,0:T(8,128)}, u32[]{:S(2)}) copy-start(f32[16,16,128]{2,1,0:T(8,128)} %param.9) | copy-start | bytes 393220
  0.0 53.6 %copy-start.1 = (s32[16,16,128]{2,1,0:T(8,128)S(1)}, s32[16,16,128]{2,1,0:T(8,128)}, u32[]{:S(2)}) copy-start(s32[16,16,128]{2,1,0:T(8,128)} %param.8) | copy-start | bytes 393220
  0.8 13.9 %collective-permute-start.1 = (f32[1,16,128]{2,1,0:T(8,128)S(1)}, f32[1,16,128]{2,1,0:T(8,128)S(1)}, u32[]{:S(2)}, u32[]{:S(2)}) collective-permute-start(f32[1,16,128]{2,1,0:T(8,128)S(1)} %get-tuple-element.43), channel_id=1, source_target_pairs={{0,1},{1,2},{2,3},{3,4},{4,5},{5,6},{6,7},{8,9},{9,10},{10,11},{11... | collective-permute-start | bytes 24584 | tf_op jit(solution)/shard_map/ppermute | solution.py:22
  6.1 8.5 %collective-permute-start = (f32[1,16,128]{2,1,0:T(8,128)S(1)}, f32[1,16,128]{2,1,0:T(8,128)S(1)}, u32[]{:S(2)}, u32[]{:S(2)}) collective-permute-start(f32[1,16,128]{2,1,0:T(8,128)S(1)} %get-tuple-element.44), channel_id=1, source_target_pairs={{1,0},{2,1},{3,2},{4,3},{5,4},{6,5},{7,6},{9,8},{10,9},{11,10},{12... | collective-permute-start | bytes 24584 | tf_op jit(solution)/shard_map/ppermute | solution.py:25
  27.7 4.3 collective-permute-start.3
  29.6 5.0 collective-permute-start.2
  46.5 4.3 collective-permute-start.5
  48.5 5.0 collective-permute-start.4
  64.4 4.3 collective-permute-start.7
  66.4 5.4 %collective-permute-start.6 = (f32[1,16,128]{2,1,0:T(8,128)S(1)}, f32[1,16,128]{2,1,0:T(8,128)S(1)}, u32[]{:S(2)}, u32[]{:S(2)}) collective-permute-start(f32[1,16,128]{2,1,0:T(8,128)S(1)} %get-tuple-element.38), channel_id=1, source_target_pairs={{1,0},{2,1},{3,2},{4,3},{5,4},{6,5},{7,6},{9,8},{10,9},{11,10},{12... | collective-permute-start | bytes 24584 | tf_op jit(solution)/shard_map/ppermute | solution.py:25
  82.7 4.5 collective-permute-start.9
  84.7 92.0 %copy-start.2 = (f32[1,16,16,128]{3,2,1,0:T(8,128)S(1)}, f32[1,16,16,128]{3,2,1,0:T(8,128)}, u32[]{:S(2)}) copy-start(f32[1,16,16,128]{3,2,1,0:T(8,128)} %param.7) | copy-start | bytes 393220
  84.7 5.1 %collective-permute-start.8 = (f32[1,16,128]{2,1,0:T(8,128)S(1)}, f32[1,16,128]{2,1,0:T(8,128)S(1)}, u32[]{:S(2)}, u32[]{:S(2)}) collective-permute-start(f32[1,16,128]{2,1,0:T(8,128)S(1)} %get-tuple-element.36), channel_id=1, source_target_pairs={{1,0},{2,1},{3,2},{4,3},{5,4},{6,5},{7,6},{9,8},{10,9},{11,10},{12... | collective-permute-start | bytes 24584 | tf_op jit(solution)/shard_map/ppermute | solution.py:25
  100.8 4.3 collective-permute-start.11
  102.7 5.0 collective-permute-start.10
  118.6 4.3 collective-permute-start.13
  120.6 5.0 collective-permute-start.12
  136.5 4.3 collective-permute-start.15
  138.5 5.0 collective-permute-start.14
  154.4 4.3 collective-permute-start.17
  156.4 5.0 collective-permute-start.16
  172.3 12.6 %collective-permute-start.19 = (f32[1,16,128]{2,1,0:T(8,128)S(1)}, f32[1,16,128]{2,1,0:T(8,128)S(1)}, u32[]{:S(2)}, u32[]{:S(2)}) collective-permute-start(f32[1,16,128]{2,1,0:T(8,128)S(1)} %get-tuple-element.25), channel_id=1, source_target_pairs={{0,1},{1,2},{2,3},{3,4},{4,5},{5,6},{6,7},{8,9},{9,10},{10,11},{11... | collective-permute-start | bytes 24584 | tf_op jit(solution)/shard_map/ppermute | solution.py:22
  174.3 10.7 %collective-permute-start.18 = (f32[1,16,128]{2,1,0:T(8,128)S(1)}, f32[1,16,128]{2,1,0:T(8,128)S(1)}, u32[]{:S(2)}, u32[]{:S(2)}) collective-permute-start(f32[1,16,128]{2,1,0:T(8,128)S(1)} %get-tuple-element.26), channel_id=1, source_target_pairs={{1,0},{2,1},{3,2},{4,3},{5,4},{6,5},{7,6},{9,8},{10,9},{11,10},{12... | collective-permute-start | bytes 24584 | tf_op jit(solution)/shard_map/ppermute | solution.py:25
  195.9 8.3 %copy-start.3 = (f32[4,4,32]{2,1,0:T(4,128)S(1)}, f32[4,4,32]{2,1,0:T(4,128)}, u32[]{:S(2)}) copy-start(f32[4,4,32]{2,1,0:T(4,128)} %param.13) | copy-start | bytes 6148
  205.3 31.2 %all-to-all-start = ((f32[64,1,512]{2,1,0:T(1,128)}), f32[64,1,512]{2,1,0:T(1,128)S(1)}, u32[]{:S(2)}, u32[]{:S(2)}) async-start(f32[64,1,512]{2,1,0:T(1,128)} %reshape.54), calls=%async_computation | async-start | bytes 262144 | tf_op jit(solution)/shard_map/all_to_all | solution.py:13
  246.1 15.1 %collective-permute-start.20 = (f32[16,16,128]{2,1,0:T(8,128)S(1)}, f32[16,16,128]{2,1,0:T(8,128)S(1)}, u32[]{:S(2)}, u32[]{:S(2)}) collective-permute-start(f32[16,16,128]{2,1,0:T(8,128)S(1)} %add.550), channel_id=1, source_target_pairs={{504,0},{0,8},{8,16},{16,24},{24,32},{32,40},{40,48},{48,56},{56,6... | collective-permute-start | bytes 393224 | tf_op jit(solution)/shard_map/ppermute | solution.py:33
  261.2 6.3 %collective-permute-start.22 = (f32[1,16,128]{2,1,0:T(8,128)S(1)}, f32[1,16,128]{2,1,0:T(8,128)S(1)}, u32[]{:S(2)}, u32[]{:S(2)}) collective-permute-start(f32[1,16,128]{2,1,0:T(8,128)S(1)} %get-tuple-element.23), channel_id=1, source_target_pairs={{0,1},{1,2},{2,3},{3,4},{4,5},{5,6},{6,7},{8,9},{9,10},{10,11},{11... | collective-permute-start | bytes 24584 | tf_op jit(solution)/shard_map/ppermute | solution.py:22
  265.6 5.0 collective-permute-start.21
  281.6 4.3 collective-permute-start.24
  283.8 5.6 %collective-permute-start.23 = (f32[1,16,128]{2,1,0:T(8,128)S(1)}, f32[1,16,128]{2,1,0:T(8,128)S(1)}, u32[]{:S(2)}, u32[]{:S(2)}) collective-permute-start(f32[1,16,128]{2,1,0:T(8,128)S(1)} %get-tuple-element.22), channel_id=1, source_target_pairs={{1,0},{2,1},{3,2},{4,3},{5,4},{6,5},{7,6},{9,8},{10,9},{11,10},{12... | collective-permute-start | bytes 24584 | tf_op jit(solution)/shard_map/ppermute | solution.py:25
  300.4 4.3 collective-permute-start.26
  302.3 5.0 collective-permute-start.25
  318.3 4.3 collective-permute-start.28
  320.2 5.0 collective-permute-start.27
  336.1 4.3 collective-permute-start.30
  338.1 5.0 collective-permute-start.29
  354.0 4.3 collective-permute-start.32
  356.0 5.0 collective-permute-start.31
  371.9 4.3 collective-permute-start.34
  373.9 5.0 collective-permute-start.33
  389.8 4.3 collective-permute-start.36
  391.8 5.0 collective-permute-start.35
  407.7 4.3 collective-permute-start.38
  409.7 5.0 collective-permute-start.37
  425.6 12.9 %collective-permute-start.40 = (f32[1,16,128]{2,1,0:T(8,128)S(1)}, f32[1,16,128]{2,1,0:T(8,128)S(1)}, u32[]{:S(2)}, u32[]{:S(2)}) collective-permute-start(f32[1,16,128]{2,1,0:T(8,128)S(1)} %get-tuple-element.5), channel_id=1, source_target_pairs={{0,1},{1,2},{2,3},{3,4},{4,5},{5,6},{6,7},{8,9},{9,10},{10,11},{11... | collective-permute-start | bytes 24584 | tf_op jit(solution)/shard_map/ppermute | solution.py:22
  427.6 10.9 %collective-permute-start.39 = (f32[1,16,128]{2,1,0:T(8,128)S(1)}, f32[1,16,128]{2,1,0:T(8,128)S(1)}, u32[]{:S(2)}, u32[]{:S(2)}) collective-permute-start(f32[1,16,128]{2,1,0:T(8,128)S(1)} %get-tuple-element.6), channel_id=1, source_target_pairs={{1,0},{2,1},{3,2},{4,3},{5,4},{6,5},{7,6},{9,8},{10,9},{11,10},{12... | collective-permute-start | bytes 24584 | tf_op jit(solution)/shard_map/ppermute | solution.py:25
  486.0 16.3 %collective-permute-start.41 = (f32[16,16,128]{2,1,0:T(8,128)S(1)}, f32[16,16,128]{2,1,0:T(8,128)S(1)}, u32[]{:S(2)}, u32[]{:S(2)}) collective-permute-start(f32[16,16,128]{2,1,0:T(8,128)S(1)} %add.621), channel_id=1, source_target_pairs={{504,0},{0,8},{8,16},{16,24},{24,32},{32,40},{40,48},{48,56},{56,6... | collective-permute-start | bytes 393224 | tf_op jit(solution)/shard_map/ppermute | solution.py:33
